TPU v7x, 512 devices: a whole 4x4x16 slice. The times are simulated.
512 devices in a mesh: ka: 16 (over y, z_hi), row: 4 (over x), col: 8 (over z_lo, core).
Axes of the slice: x: 4, y: 4, z: 16 (z_hi: 4, z_lo: 4; z = z_hi * 4 + z_lo), core: 2. Of those that a mesh axis runs over, the one named last changes fastest.
Arguments:
- exciton: bfloat16 [16, 4, 128, 128], P('ka'), may hold values from -6 to 6
- orb_cond: bfloat16 [16, 128, 2048], P('ka', None, 'row'), may hold values from -0.5 to 0.5
- orb_val: bfloat16 [16, 128, 2048], P('ka', None, 'col'), may hold values from -0.5 to 0.5
- screened: bfloat16 [16, 2048, 2048], P(None, 'row', 'col'), may hold values from -1.5 to 1.5
- q_table: int32 [16, 16], replicated, may hold values from 0 to 15, as said below
Outputs:
- applied: float32 [16, 4, 128, 128], P('ka', None, 'col')
Inputs may be any that keep to these rules, and one draw needn't show every extreme that they name: q_table is the difference table of the k-points of a cyclic grid of 16 points under a relabeling of points and of differences: every row and every column holds each of 0 to 15 once.
All inputs are finite; a program needn't handle non-finite values.
Results may differ from a plain program's by a relative error of at most 0.019.
Values may be sent and summed in bfloat16 or wider, within the bound.
A program may use at most 64 MiB of HBM per device.

v0:
```python
import math
import jax
import jax.numpy as jnp
from jax import lax
from jax.sharding import PartitionSpec as P

NV = 128
NC = 128
NMU = 2048


def split_up(x, dim, devices):
    before, after = (x.shape[:dim], x.shape[dim + 1 :])
    return jnp.moveaxis(x.reshape(*before, devices, -1, *after), dim, 0)


def summed_on_arrival(x, axis, dim):
    blocks = split_up(x, dim, lax.axis_size(axis))
    arrived = lax.all_to_all(blocks, axis, split_axis=0, concat_axis=0, tiled=True)
    return arrived.astype(jnp.float32).sum(axis=0)


def copy_for_each(x, axis):
    devices = lax.axis_size(axis)
    return lax.all_to_all(jnp.broadcast_to(x[None], (devices, *x.shape)), axis, 0, 0, tiled=True)


def of_everyone(x, axis):
    return copy_for_each(x, axis).astype(jnp.float32).sum(axis=0)


def local(exciton, orb_cond, orb_val, screened, q_table):
    local_count = exciton.shape[0]
    own_points = lax.axis_index("ka") * local_count + jnp.arange(local_count, dtype=jnp.int32)
    q_columns = jnp.take(q_table, own_points, axis=1)
    panels = jnp.einsum(
        "kbvc,kcm->kbvm", exciton, orb_cond, preferred_element_type=jnp.float32
    ).astype(jnp.bfloat16)
    start_sum = jnp.zeros(
        (local_count, exciton.shape[1], orb_cond.shape[2], orb_val.shape[2]), jnp.float32
    )

    def weigh_pairs(running, pair_block, position):
        indices = lax.dynamic_index_in_dim(q_columns, position, 0, keepdims=False)
        weights = jnp.take(screened, indices, axis=0).astype(jnp.float32)
        return running + weights[:, None] * pair_block[None].astype(jnp.float32)

    portion = (
        lax.all_gather(panels, "ka", axis=0, tiled=True),
        lax.all_gather(orb_val, "ka", axis=0, tiled=True),
    )

    def one_point(entry_index, inner_sum):
        panel_rows = lax.dynamic_index_in_dim(portion[0], entry_index, 0, keepdims=False)
        valence = lax.dynamic_index_in_dim(portion[1], entry_index, 0, keepdims=False)
        pair_block = jnp.einsum(
            "bvm,vn->bmn", panel_rows, valence, preferred_element_type=jnp.float32
        ).astype(jnp.bfloat16)
        return weigh_pairs(inner_sum, pair_block, entry_index)

    direct = lax.fori_loop(0, portion[0].shape[0], one_point, start_sum)
    direct = direct.astype(jnp.bfloat16)
    half_sums = jnp.einsum(
        "kbmn,kvn->kbmv", direct, orb_val, preferred_element_type=jnp.float32
    ).astype(jnp.bfloat16)
    factor = math.sqrt(NV * NC) / NMU
    partial_value = (
        jnp.einsum("kcm,kbmv->kbvc", orb_cond, half_sums, preferred_element_type=jnp.float32)
        * factor
    )
    shares = summed_on_arrival(partial_value.astype(jnp.bfloat16), "col", 2)
    result = of_everyone(shares.astype(jnp.bfloat16), "row").astype(jnp.float32)
    return result


def solution(mesh):
    placed = (
        P("ka", None, None, None),
        P("ka", None, "row"),
        P("ka", None, "col"),
        P(None, "row", "col"),
        P(),
    )
    return jax.shard_map(
        local, mesh=mesh, in_specs=placed, out_specs=P("ka", None, "col", None), check_vma=False
    )
```

profile of v0, /device:TPU:8, one launch (start us, length us, event | category | flops | bytes accessed | tf_op | source)
XLA Modules:
  0.0 422.1 jit_solution(8037367269032499573)
XLA Ops:
  7.4 2.0 convolution_convert_fusion.2
  10.3 81.8 %all-gather.4.cloned.1.call-done = bf16[16,128,256]{2,1,0:T(8,128)(2,1)} async-done(((bf16[1,128,256]{2,1,0:T(8,128)(2,1)}), bf16[16,128,256]{2,1,0:T(8,128)(2,1)}) %all-gather.4.cloned.1.call-update) | async-done | bytes 1048592 | tf_op jit(solution)/shard_map/all_gather | solution.py:50
  92.1 215.3 %all-gather.6.cloned.1.call-done = bf16[64,128,512]{2,1,0:T(8,128)(2,1)} async-done(((bf16[4,128,512]{2,1,0:T(8,128)(2,1)}), bf16[64,128,512]{2,1,0:T(8,128)(2,1)}) %all-gather.6.cloned.1.call-update) | async-done | bytes 8388624 | tf_op jit(solution)/shard_map/all_gather | solution.py:49
  307.4 86.6 %while.16 = (s32[]{:T(128)}, f32[1,4,512,256]{3,2,1,0:T(8,128)S(1)}, s32[16,1]{0,1:T(1,128)S(1)}, bf16[16,512,256]{2,1,0:T(8,128)(2,1)}, bf16[16,4,128,512]{3,2,...) while((s32[]{:T(128)}, ...), condition=%wide.region_1.2_spmd.clone, body=%wide.region_0.1_spmd.clone.sunk | while | flops 137101312 | bytes 6096063 | solution.py:61
  309.9 1.0 bitcast_convert_fusion.2
  310.9 1.9 bitcast_add_fusion.2
  315.3 1.0 bitcast_convert_fusion.2
  316.3 1.9 bitcast_add_fusion.2
  320.7 1.0 bitcast_convert_fusion.2
  321.7 1.9 bitcast_add_fusion.2
  326.2 1.0 bitcast_convert_fusion.2
  327.2 1.9 bitcast_add_fusion.2
  331.6 1.0 bitcast_convert_fusion.2
  332.6 1.9 bitcast_add_fusion.2
  338.0 1.9 bitcast_add_fusion.2
  343.4 1.9 bitcast_add_fusion.2
  348.8 1.9 bitcast_add_fusion.2
  353.2 1.0 bitcast_convert_fusion.2
  354.2 1.9 bitcast_add_fusion.2
  358.7 1.0 bitcast_convert_fusion.2
  359.7 1.9 bitcast_add_fusion.2
  364.1 1.0 bitcast_convert_fusion.2
  365.1 1.9 bitcast_add_fusion.2
  369.5 1.0 bitcast_convert_fusion.2
  370.5 1.9 bitcast_add_fusion.2
  375.9 1.9 bitcast_add_fusion.2
  381.3 1.9 bitcast_add_fusion.2
  385.7 1.0 bitcast_convert_fusion.2
  386.7 1.9 bitcast_add_fusion.2
  392.1 1.9 bitcast_add_fusion.2
  395.0 10.0 %all_to_all.10 = bf16[8,1,4,16,128]{4,3,2,1,0:T(8,128)(2,1)S(1)} all-to-all(bf16[8,1,4,16,128]{4,3,2,1,0:T(8,128)(2,1)S(1)} %bitcast.59), channel_id=1, replica_groups=mesh['ka'=16,'row'=4,'col'=8] {'col'}, dimensions={0} | all-to-all | bytes 262144 | tf_op jit(solution)/shard_map/all_to_all | solution.py:19
  405.0 9.7 %all_to_all.11 = bf16[4,1,4,16,128]{4,3,2,1,0:T(8,128)(2,1)S(1)} all-to-all(bf16[4,1,4,16,128]{4,3,2,1,0:T(8,128)(2,1)S(1)} %broadcast_in_dim.46), channel_id=1, replica_groups=mesh['ka'=16,'row'=4,'col'=8] {'row'}, dimensions={0} | all-to-all | bytes 131072 | tf_op jit(solution)/shard_map/all_to_all | solution.py:25
  (39 shorter events, 18.8 us)
Async XLA Ops:
  6.5 0.9 copy-start
  6.5 85.6 %all-gather.4.cloned.1.call-start = ((), (), s32[]{:S(2)}) async-start(), calls=%async_computation.2 | async-start | bytes 1114112 | tf_op jit(solution)/shard_map/all_gather | solution.py:50
  7.3 300.2 %all-gather.6.cloned.1.call-start = ((), (), s32[]{:S(2)}) async-start(), calls=%async_computation.3 | async-start | bytes 8912896 | tf_op jit(solution)/shard_map/all_gather | solution.py:49
  307.4 86.6 %copy-start.1 = (bf16[1,128,256]{2,1,0:T(8,128)(2,1)S(1)}, bf16[1,128,256]{2,1,0:T(8,128)(2,1)}, u32[]{:S(2)}) copy-start(bf16[1,128,256]{2,1,0:T(8,128)(2,1)} %param.9) | copy-start | bytes 196612
Sparse Core Ops, SparseCore 0:
  10.3 81.7 all-gather.3
  95.1 212.2 all-gather.5
where the time goes:
time: 424 us; the launch traced here: 422 us
  waiting for transfers between devices  298 us (70%)
  matrix products  33.4 us (8%)
  loops' own time  30.6 us (7%)
  blocking collectives  19.7 us (5%)
  other arithmetic  16.5 us (4%)
  between operations  13.5 us (3%)
  local copies, waits for them, and re-layouts  10.5 us (2%)
    all_gather x1, waiting for transfers between devices, local(): lax.all_gather(panels, 'ka', axis=0, tiled=True)  215 us
    all_gather x1, waiting for transfers between devices, local(): lax.all_gather(orb_val, 'ka', axis=0, tiled=True)  81.8 us
    dot_general x16, matrix products, one_point(): jnp.einsum('bvm,vn->bmn', panel_rows, valence, preferred_element_type=jnp...  30.6 us
    another operation x1, loops' own time, local(): direct = lax.fori_loop(0, portion[0].shape[0], one_point, start_sum)  30.6 us
    convert_element_type x16, other arithmetic, weigh_pairs(): weights = jnp.take(screened, indices, axis=0).astype(jnp.float32)  15.9 us
    all_to_all x1, blocking collectives, summed_on_arrival(): lax.all_to_all(blocks, axis, split_axis=0, concat_axis=0, tiled=True)  9.99 us
    all_to_all x1, blocking collectives, copy_for_each(): lax.all_to_all(jnp.broadcast_to(x[None], (devices, *x.shape)), axis, 0, 0...  9.67 us
    dynamic_slice x16, local copies, waits for them, and re-layouts, weigh_pairs(): indices = lax.dynamic_index_in_dim(q_columns, position, 0, keepdims=False)  9.52 us
  transfers between devices with their start and end apart: 2, of which 2 were waited for; matrix products, arithmetic and copies ran while one was open for 1% of the time, Pallas kernels for 0%

commit v1 on v0

--- a/solution.py
+++ b/solution.py
@@ -46,7 +46,9 @@
         return running + weights[:, None] * pair_block[None].astype(jnp.float32)
 
     portion = (
-        lax.all_gather(panels, "ka", axis=0, tiled=True),
+        jnp.concatenate(
+            lax.all_to_all(jnp.stack([panels] * lax.axis_size("ka")), "ka", 0, 0), axis=0
+        ),
         lax.all_gather(orb_val, "ka", axis=0, tiled=True),
     )
 

time: 424 us -> 551 us (1.30)
  waiting for transfers between devices: 298 us -> 386 us
  starting transfers between devices: 0.04 us -> 18.3 us
  blocking collectives: 19.7 us -> 34.2 us
  local copies, waits for them, and re-layouts: 10.5 us -> 17.1 us
    all_gather x1 -> x0, waiting for transfers between devices: 215 us -> none  [local(): lax.all_gather(panels, 'ka', axis=0, tiled=True)]
    all_to_all x0 -> x1, waiting for transfers between devices: none -> 205 us  [local(): lax.all_to_all(jnp.stack([panels] * lax.axis_size('ka')), 'ka', 0, 0)]
    all_gather x1, waiting for transfers between devices: 81.8 us -> 181 us  [local(): lax.all_gather(orb_val, 'ka', axis=0, tiled=True)]
    all_to_all x0 -> x1, starting transfers between devices: none -> 18.3 us  [local(): lax.all_to_all(jnp.stack([panels] * lax.axis_size('ka')), 'ka', 0, 0)]
    all_to_all x1, blocking collectives: 9.99 us -> 18.8 us  [summed_on_arrival(): lax.all_to_all(blocks, axis, split_axis=0, concat_axis=0, tiled=True)]
    all_to_all x1, blocking collectives: 9.67 us -> 15.4 us  [copy_for_each(): lax.all_to_all(jnp.broadcast_to(x[None], (devices, *x.shape)), axis, 0, 0...]
  transfers between devices with their start and end apart: 2 -> 2, of which waited for: 2 -> 2; matrix products, arithmetic and copies ran while one was open for 1% -> 0% of each run, Pallas kernels for 0% -> 0%
where the time goes in v1:
time: 551 us; the launch traced here: 550 us
  waiting for transfers between devices  386 us (70%)
  blocking collectives  34.2 us (6%)
  loops' own time  33.1 us (6%)
  matrix products  30.9 us (6%)
  starting transfers between devices  18.3 us (3%)
  local copies, waits for them, and re-layouts  17.1 us (3%)
  other arithmetic  16.5 us (3%)
  between operations  13.5 us (2%)
    all_to_all x1, waiting for transfers between devices, local(): lax.all_to_all(jnp.stack([panels] * lax.axis_size('ka')), 'ka', 0, 0)  205 us
    all_gather x1, waiting for transfers between devices, local(): lax.all_gather(orb_val, 'ka', axis=0, tiled=True)  181 us
    another operation x1, loops' own time, local(): direct = lax.fori_loop(0, portion[0].shape[0], one_point, start_sum)  33.1 us
    dot_general x16, matrix products, one_point(): jnp.einsum('bvm,vn->bmn', panel_rows, valence, preferred_element_type=jnp...  28.9 us
    all_to_all x1, blocking collectives, summed_on_arrival(): lax.all_to_all(blocks, axis, split_axis=0, concat_axis=0, tiled=True)  18.8 us
    all_to_all x1, starting transfers between devices, local(): lax.all_to_all(jnp.stack([panels] * lax.axis_size('ka')), 'ka', 0, 0)  18.3 us
    convert_element_type x16, other arithmetic, weigh_pairs(): weights = jnp.take(screened, indices, axis=0).astype(jnp.float32)  15.9 us
    all_to_all x1, blocking collectives, copy_for_each(): lax.all_to_all(jnp.broadcast_to(x[None], (devices, *x.shape)), axis, 0, 0...  15.4 us
  transfers between devices with their start and end apart: 2, of which 2 were waited for; matrix products, arithmetic and copies ran while one was open for 0% of the time, Pallas kernels for 0%

profile of v1, /device:TPU:8, one launch (start us, length us, event | category | flops | bytes accessed | tf_op | source)
XLA Modules:
  0.0 549.6 jit_solution(11455147473228186166)
XLA Ops:
  7.4 1.2 convolution_convert_fusion.2
  8.9 5.3 stack.2
  14.2 18.3 %all-to-all-start = ((bf16[16,1,4,128,512]{3,4,2,1,0:T(8,128)(2,1)}), bf16[16,1,4,128,512]{3,4,2,1,0:T(8,128)(2,1)}, u32[]{:S(2)}, u32[]{:S(2)}) async-start(bf16[16,1,4,128,512]{3,4,2,1,0:T(8,128)(2,1)} %stack.2), calls=%async_computation | async-start | bytes 16777216 | tf_op jit(solution)/shard_map/all_to_all | solution.py:50
  33.5 180.5 %all-gather.2.cloned.1.call-done = bf16[16,128,256]{2,1,0:T(8,128)(2,1)} async-done(((bf16[1,128,256]{2,1,0:T(8,128)(2,1)}), bf16[16,128,256]{2,1,0:T(8,128)(2,1)}) %all-gather.2.cloned.1.call-update) | async-done | bytes 1048592 | tf_op jit(solution)/shard_map/all_gather | solution.py:52
  214.0 204.6 %all-to-all-done = bf16[16,1,4,128,512]{3,4,2,1,0:T(8,128)(2,1)} async-done(((bf16[16,1,4,128,512]{3,4,2,1,0:T(8,128)(2,1)}), bf16[16,1,4,128,512]{3,4,2,1,0:T(8,128)(2,1)}, u32[]{:S(2)}, u32[]{:S(2)}) %all-to-all-start) | async-done | bytes 8388640 | tf_op jit(solution)/shard_map/all_to_all | solution.py:50
  418.6 88.3 %while.16 = (s32[]{:T(128)}, f32[1,4,512,256]{3,2,1,0:T(8,128)S(1)}, s32[16,1]{0,1:T(1,128)S(1)}, bf16[16,512,256]{2,1,0:T(8,128)(2,1)}, bf16[16,4,128,512]{2,3,...) while((s32[]{:T(128)}, ...), condition=%wide.region_1.2_spmd.clone, body=%wide.region_0.1_spmd.clone.sunk | while | flops 137101312 | bytes 6096063 | solution.py:63
  422.3 1.8 bitcast_add_fusion.2
  427.9 1.8 bitcast_add_fusion.2
  433.4 1.8 bitcast_add_fusion.2
  437.9 1.0 bitcast_convert_fusion.2
  438.9 1.8 bitcast_add_fusion.2
  443.4 1.0 bitcast_convert_fusion.2
  444.4 1.8 bitcast_add_fusion.2
  448.9 1.0 bitcast_convert_fusion.2
  449.9 1.8 bitcast_add_fusion.2
  454.5 1.0 bitcast_convert_fusion.2
  455.5 1.8 bitcast_add_fusion.2
  460.0 1.0 bitcast_convert_fusion.2
  461.0 1.8 bitcast_add_fusion.2
  465.5 1.0 bitcast_convert_fusion.2
  466.5 1.8 bitcast_add_fusion.2
  471.0 1.0 bitcast_convert_fusion.2
  472.0 1.8 bitcast_add_fusion.2
  476.5 1.0 bitcast_convert_fusion.2
  477.5 1.8 bitcast_add_fusion.2
  483.1 1.8 bitcast_add_fusion.2
  488.6 1.8 bitcast_add_fusion.2
  494.1 1.8 bitcast_add_fusion.2
  499.6 1.8 bitcast_add_fusion.2
  505.1 1.8 bitcast_add_fusion.2
  507.8 18.8 %all_to_all.15 = bf16[8,1,4,16,128]{4,3,2,1,0:T(8,128)(2,1)S(1)} all-to-all(bf16[8,1,4,16,128]{4,3,2,1,0:T(8,128)(2,1)S(1)} %bitcast.57), channel_id=1, replica_groups=mesh['ka'=16,'row'=4,'col'=8] {'col'}, dimensions={0} | all-to-all | bytes 262144 | tf_op jit(solution)/shard_map/all_to_all | solution.py:19
  526.7 15.4 %all_to_all.16 = bf16[4,1,4,16,128]{4,3,2,1,0:T(8,128)(2,1)S(1)} all-to-all(bf16[4,1,4,16,128]{4,3,2,1,0:T(8,128)(2,1)S(1)} %broadcast_in_dim.46), channel_id=1, replica_groups=mesh['ka'=16,'row'=4,'col'=8] {'row'}, dimensions={0} | all-to-all | bytes 131072 | tf_op jit(solution)/shard_map/all_to_all | solution.py:25
  (42 shorter events, 21.9 us)
Async XLA Ops:
  6.5 0.9 copy-start
  14.2 19.1 %copy-start.2 = (s32[16,16]{1,0:T(8,128)S(1)}, s32[16,16]{1,0:T(8,128)}, u32[]{:S(2)}) copy-start(s32[16,16]{1,0:T(8,128)} %param.11) | copy-start | bytes 3076
  14.2 404.4 %all-to-all-start = ((bf16[16,1,4,128,512]{3,4,2,1,0:T(8,128)(2,1)}), bf16[16,1,4,128,512]{3,4,2,1,0:T(8,128)(2,1)}, u32[]{:S(2)}, u32[]{:S(2)}) async-start(bf16[16,1,4,128,512]{3,4,2,1,0:T(8,128)(2,1)} %stack.2), calls=%async_computation | async-start | bytes 16777216 | tf_op jit(solution)/shard_map/all_to_all | solution.py:50
  32.5 181.5 %all-gather.2.cloned.1.call-start = ((), (), s32[]{:S(2)}) async-start(), calls=%async_computation.3 | async-start | bytes 1114112 | tf_op jit(solution)/shard_map/all_gather | solution.py:52
  418.6 88.3 %copy-start.1 = (bf16[1,128,256]{2,1,0:T(8,128)(2,1)S(1)}, bf16[1,128,256]{2,1,0:T(8,128)(2,1)}, u32[]{:S(2)}) copy-start(bf16[1,128,256]{2,1,0:T(8,128)(2,1)} %param.9) | copy-start | bytes 196612
Sparse Core Ops, SparseCore 0:
  36.4 177.5 all-gather.1
